TPU v7x, 256 devices: a whole 4x4x8 slice. The times are simulated.
256 devices in a mesh: grp: 8 (over x, core), mem: 32 (over y, z).
Axes of the slice: x: 4, y: 4, z: 8, core: 2. Of those that a mesh axis runs over, the one named last changes fastest.
Arguments:
- child_field: float32 [2, 1024, 32768], P(None, None, ('grp', 'mem')), may hold values from -6 to 6
- theta_interp: float32 [64, 32], replicated, may hold values from -1 to 1
- phi_interp: float32 [64, 32], replicated, may hold values from -1 to 1
- child_phase: float32 [8, 4096], replicated, may hold values from -3.140625 to 3.140625
- translation: float32 [2, 316, 4096], P(None, None, 'mem'), may hold values from -0.3125 to 0.3125
- inter_source: int32 [256, 24], P('grp'), may hold values from 0 to 255, as said below
- inter_kind: int32 [256, 24], P('grp'), may hold values from 0 to 315
- inter_count: int32 [256], P('grp'), may hold values from 6 to 24
Outputs:
- child_out: float32 [2, 1024, 32768], P(None, None, ('grp', 'mem'))
Inputs may be any that keep to these rules, and one draw needn't show every extreme that they name: The source box of every slot lies in its target's group of 32 consecutive parent boxes or in one of the two groups beside it: inter_source[t, k] // 32 differs from t // 32 by at most one. Slots from inter_count[t] on are unused.
All inputs are finite; a program needn't handle non-finite values.
Results may differ from a plain program's by a relative error of at most 0.0003.
Values sent between devices are 32-bit elements; how exact they have to be, the bound alone decides.
A program may use at most 64 MiB of HBM per device.

v0:
```python
import functools
import math

import jax
import jax.numpy as jnp
from jax import lax
from jax.experimental import pallas as pl
from jax.experimental.pallas import tpu as pltpu
from jax.sharding import PartitionSpec as P

MESH = pl.DeviceIdType.MESH
f32 = jnp.float32
bf16 = jnp.bfloat16


def two_terms(x):
    high = x.astype(bf16)
    return high, (x - high.astype(f32)).astype(bf16)


def dot(a, b):
    return jnp.dot(a, b, preferred_element_type=f32)


def dot_rows(a, b):
    return lax.dot_general(a, b, (((1,), (1,)), ((), ())), preferred_element_type=f32)


def where_true(rows, cols, test):
    r = lax.broadcasted_iota(jnp.int32, (rows, cols), 0)
    c = lax.broadcasted_iota(jnp.int32, (rows, cols), 1)
    return jnp.where(test(r, c), 1.0, 0.0).astype(f32)


def sine_and_cosine(q):
    y = 0.5 * q
    z = y * y
    s = 0.0
    for n in (11, 9, 7, 5, 3, 1):
        s = s * z + (-1.0) ** (n // 2) / math.factorial(n)
    c = 0.0
    for n in (12, 10, 8, 6, 4, 2, 0):
        c = c * z + (-1.0) ** (n // 2) / math.factorial(n)
    s = s * y
    return 2.0 * s * c, 1.0 - 2.0 * s * s


def body(
    dims,
    x_ref,
    theta_ref,
    phi_ref,
    phase_ref,
    trans_ref,
    source_ref,
    kind_ref,
    count_ref,
    out_ref,
    cos_ref,
    sin_ref,
    mid_ref,
    back_ref,
    spread_lhs,
    spread_rhs,
    fold_lhs,
    fold_rhs,
    table_ref,
    give_ref,
    hold_ref,
    result_ref,
    take_ref,
    give_sem,
    hold_sem,
    pass_sem,
    side_sem,
    result_sem,
    take_sem,
):
    groups, members, coarse_t, coarse_p, fine_t, fine_p, branch, waves, slots, kinds = dims
    pairs = members // 2
    lanes = 2 * fine_p
    columns = branch * waves
    me = lax.axis_index("mem")
    group = lax.axis_index("grp")
    right = lax.rem(group + 1, groups)
    left = lax.rem(group + groups - 1, groups)

    barrier = pltpu.get_barrier_semaphore()

    def greet(k, carry):
        pl.semaphore_signal(
            barrier, inc=1, device_id={"mem": lax.rem(me + k, members)}, device_id_type=MESH
        )
        return carry

    lax.fori_loop(1, members, greet, 0)
    for other in (left, right):
        pl.semaphore_signal(barrier, inc=1, device_id={"grp": other}, device_id_type=MESH)

    def pair_at(k, sign):
        if pairs == 16:
            step = lax.rem(11 * (k + 1), 16)
            home = me // 2
            y = lax.rem(home // 4 + 4 + sign * (step // 4), 4)
            z = lax.rem(lax.rem(home, 4) + 4 + sign * lax.rem(step, 4), 4)
            return 4 * y + z
        return lax.rem(me // 2 + pairs + sign * lax.rem(k + 1, pairs), pairs)

    theta_high, theta_low = two_terms(theta_ref[...])
    phi_high, phi_low = two_terms(phi_ref[...])
    at = lambda rows, cols, test: where_true(rows, cols, test).astype(bf16)
    spread_lhs[...] = (
        dot(theta_high, at(coarse_t, 3 * coarse_t, lambda r, c: (c == r) | (c == r + coarse_t)))
        + dot(theta_low, at(coarse_t, 3 * coarse_t, lambda r, c: c == r + 2 * coarse_t))
    ).astype(bf16)
    own = where_true(4 * coarse_p, 4 * fine_p, lambda r, c: r // coarse_p == c // fine_p)
    rows_p = at(4 * coarse_p, coarse_p, lambda r, c: (r & (coarse_p - 1)) == c)
    cols_b = at(fine_p, 4 * fine_p, lambda r, c: r == (c & (fine_p - 1)))
    for n, term in enumerate((phi_high, phi_low)):
        small = dot_rows(rows_p, term).astype(bf16)
        spread_rhs[n] = (dot(small, cols_b) * own).astype(bf16)

    def angles(i, carry):
        at_lanes = pl.ds(pl.multiple_of(i * 2 * lanes, 2 * lanes), 2 * lanes)
        s, c = sine_and_cosine(phase_ref[:, at_lanes])
        sin_ref[:, at_lanes] = s
        cos_ref[:, at_lanes] = c
        return carry

    lax.fori_loop(0, pairs, angles, 0)

    lhs = spread_lhs[...]

    def theta_step(p, carry):
        terms = [two_terms(x_ref[n, pl.ds(p, coarse_t, stride=coarse_p), :]) for n in range(2)]
        high = jnp.concatenate([terms[0][0], terms[1][0]], axis=1)
        low = jnp.concatenate([terms[0][1], terms[1][1]], axis=1)
        made = dot(lhs, jnp.concatenate([high, low, high], axis=0))
        for n in range(2):
            mid_ref[n, pl.ds(p, fine_t, stride=coarse_p), :] = made[
                :, n * columns : (n + 1) * columns
            ]
        return carry

    lax.fori_loop(0, coarse_p, theta_step, 0, unroll=8)

    pl.semaphore_wait(barrier, members + 1)

    def give_copy(to):
        return pltpu.make_async_remote_copy(
            src_ref=give_ref.at[to],
            dst_ref=hold_ref.at[members + me],
            send_sem=give_sem.at[to],
            recv_sem=hold_sem.at[me],
            device_id={"mem": to},
            device_id_type=MESH,
        )

    def spread_pair(k, carry):
        pair = pair_at(k, 1)
        rows = pl.ds(pl.multiple_of(pair * 4 * coarse_p, 4 * coarse_p), 4 * coarse_p)
        turned = jnp.concatenate([mid_ref[0, rows, :].T, mid_ref[1, rows, :].T], axis=0)
        high, low = two_terms(turned)
        both = jnp.concatenate([spread_rhs[0], spread_rhs[0]], axis=0)
        fine = dot(jnp.concatenate([high, low], axis=1), both) + dot(high, spread_rhs[1])
        at_lanes = pl.ds(pl.multiple_of(pair * 2 * lanes, 2 * lanes), 2 * lanes)
        cosine = cos_ref[:, at_lanes]
        sine = sin_ref[:, at_lanes]
        real = imag = 0.0
        for j in range(branch):
            re = fine[j * waves : (j + 1) * waves]
            im = fine[columns + j * waves : columns + (j + 1) * waves]
            c, s = cosine[j : j + 1], sine[j : j + 1]
            real = real + (re * c - im * s)
            imag = imag + (im * c + re * s)
        for side in range(2):
            to = 2 * pair + side
            cut = slice(side * lanes, (side + 1) * lanes)
            block = (real[:, cut].reshape(2, waves // 2, lanes), imag[:, cut].reshape(2, waves // 2, lanes))
            for n in range(2):
                give_ref[to, n] = block[n]

            @pl.when(to != me)
            def _():
                give_copy(to).start()

            @pl.when(to == me)
            def _():
                for n in range(2):
                    hold_ref[members + me, n] = block[n]

        return carry

    lax.fori_loop(0, pairs, spread_pair, 0)

    def table_step(i, carry):
        for n in range(2):
            table_ref[i, n] = jnp.broadcast_to(trans_ref[n, pl.ds(i, 1), :], (waves // 2, lanes))
        return carry

    lax.fori_loop(0, kinds, table_step, 0)
    table_ref[kinds] = jnp.zeros((2, waves // 2, lanes), f32)

    def pass_copy(box, way):
        to = right if way == 0 else left
        return pltpu.make_async_remote_copy(
            src_ref=hold_ref.at[members + box],
            dst_ref=hold_ref.at[2 * members * way + box],
            send_sem=pass_sem.at[way, box],
            recv_sem=side_sem.at[way],
            device_id={"grp": to},
            device_id_type=MESH,
        )

    def pass_pair(k, carry):
        pair = pair_at(k, -1)
        for side in range(2):
            box = 2 * pair + side

            @pl.when(box != me)
            def _():
                pltpu.make_async_remote_copy(
                    src_ref=give_ref.at[box],
                    dst_ref=hold_ref.at[members + box],
                    send_sem=give_sem.at[box],
                    recv_sem=hold_sem.at[box],
                    device_id={"mem": box},
                    device_id_type=MESH,
                ).wait_recv()

            for way in range(2):
                pass_copy(box, way).start()
        return carry

    lax.fori_loop(0, pairs, pass_pair, 0)

    own_back = where_true(4 * fine_p, 4 * coarse_p, lambda r, c: r // fine_p == c // coarse_p)
    rows_b = at(4 * fine_p, fine_p, lambda r, c: (r & (fine_p - 1)) == c)
    cols_p = at(coarse_p, 4 * coarse_p, lambda r, c: r == (c & (coarse_p - 1)))
    for n, term in enumerate((phi_high, phi_low)):
        small = dot(rows_b, term).astype(bf16)
        fold_rhs[:, n * 4 * coarse_p : (n + 1) * 4 * coarse_p] = (
            dot(small, cols_p) * own_back
        ).astype(bf16)
    eye = at(coarse_t, coarse_t, lambda r, c: r == c)
    turned_high = dot_rows(eye, theta_high).astype(bf16)
    turned_low = dot_rows(eye, theta_low).astype(bf16)
    fold_lhs[...] = (
        dot(turned_high, at(fine_t, 3 * fine_t, lambda r, c: (c == r) | (c == r + fine_t)))
        + dot(turned_low, at(fine_t, 3 * fine_t, lambda r, c: c == r + 2 * fine_t))
    ).astype(bf16)

    for way in range(2):
        span = pl.ds(2 * members * way, members)
        pltpu.make_async_remote_copy(
            src_ref=hold_ref.at[span],
            dst_ref=hold_ref.at[span],
            send_sem=pass_sem.at[way, 0],
            recv_sem=side_sem.at[way],
            device_id={"grp": right},
            device_id_type=MESH,
        ).wait_recv()

    base = (group - 1) * members

    def translate(k, carry):
        target = 2 * pair_at(k // 2, 1) + lax.rem(k, 2)
        live = count_ref[target]
        real = jnp.zeros((2, waves // 2, lanes), f32)
        imag = jnp.zeros((2, waves // 2, lanes), f32)
        for slot in range(slots):
            used = slot < live
            source = jnp.where(used, source_ref[target, slot] - base, members)
            kind = jnp.where(used, kind_ref[target, slot], kinds)
            box = hold_ref[source]
            factor = table_ref[kind]
            real = real + (factor[0] * box[0] - factor[1] * box[1])
            imag = imag + (factor[0] * box[1] + factor[1] * box[0])
        result_ref[target, 0] = real
        result_ref[target, 1] = imag

        @pl.when(target != me)
        def _():
            pltpu.make_async_remote_copy(
                src_ref=result_ref.at[target],
                dst_ref=take_ref.at[me],
                send_sem=result_sem.at[target],
                recv_sem=take_sem.at[me],
                device_id={"mem": target},
                device_id_type=MESH,
            ).start()

        @pl.when(target == me)
        def _():
            take_ref[me, 0] = real
            take_ref[me, 1] = imag

        return carry

    lax.fori_loop(0, members, translate, 0)

    def fold_pair(k, carry):
        pair = pair_at(k, -1)
        for side in range(2):
            box = 2 * pair + side

            @pl.when(box != me)
            def _():
                pltpu.make_async_remote_copy(
                    src_ref=result_ref.at[box],
                    dst_ref=take_ref.at[box],
                    send_sem=result_sem.at[box],
                    recv_sem=take_sem.at[box],
                    device_id={"mem": box},
                    device_id_type=MESH,
                ).wait_recv()

        at_lanes = pl.ds(pl.multiple_of(pair * 2 * lanes, 2 * lanes), 2 * lanes)
        cosine = cos_ref[:, at_lanes]
        sine = sin_ref[:, at_lanes]
        re, im = (
            jnp.concatenate(
                [take_ref[2 * pair + side, n].reshape(waves, lanes) for side in range(2)], axis=1
            )
            for n in range(2)
        )
        parts = [[], []]
        for j in range(branch):
            c, s = cosine[j : j + 1], sine[j : j + 1]
            parts[0].append(re * c + im * s)
            parts[1].append(im * c - re * s)
        high, low = two_terms(jnp.concatenate(parts[0] + parts[1], axis=0))
        wide = dot(high, fold_rhs[...])
        width = 4 * coarse_p
        made = wide[:, :width] + wide[:, width:] + dot(low, fold_rhs[:, :width])
        rows = pl.ds(pl.multiple_of(pair * width, width), width)
        for n in range(2):
            back_ref[n, rows, :] = made[n * columns : (n + 1) * columns].T
        return carry

    lax.fori_loop(0, pairs, fold_pair, 0)

    lhs_back = fold_lhs[...]

    def fold_step(p, carry):
        terms = [two_terms(back_ref[n, pl.ds(p, fine_t, stride=coarse_p), :]) for n in range(2)]
        high = jnp.concatenate([terms[0][0], terms[1][0]], axis=1)
        low = jnp.concatenate([terms[0][1], terms[1][1]], axis=1)
        made = dot(lhs_back, jnp.concatenate([high, low, high], axis=0))
        for n in range(2):
            out_ref[n, pl.ds(p, coarse_t, stride=coarse_p), :] = made[
                :, n * columns : (n + 1) * columns
            ]
        return carry

    lax.fori_loop(0, coarse_p, fold_step, 0, unroll=8)

    def sent(k, carry):
        to = lax.rem(me + k, members)
        give_copy(to).wait_send()
        pltpu.make_async_remote_copy(
            src_ref=result_ref.at[to],
            dst_ref=take_ref.at[me],
            send_sem=result_sem.at[to],
            recv_sem=take_sem.at[me],
            device_id={"mem": to},
            device_id_type=MESH,
        ).wait_send()
        return carry

    lax.fori_loop(1, members, sent, 0)

    def passed(box, carry):
        for way in range(2):
            pass_copy(box, way).wait_send()
        return carry

    lax.fori_loop(0, members, passed, 0)


def per_device(groups, members, waves, *arrays):
    field, theta, phi, phase, trans, source, kind, count = arrays
    fine_t, coarse_t = theta.shape
    fine_p, coarse_p = phi.shape
    branch = phase.shape[0]
    slots = source.shape[1]
    kinds = trans.shape[1]
    columns = field.shape[2]
    lanes = trans.shape[2]
    dims = (groups, members, coarse_t, coarse_p, fine_t, fine_p, branch, waves, slots, kinds)
    block = (2, 2, waves // 2, lanes)
    in_vmem = pl.BlockSpec(memory_space=pltpu.VMEM)
    in_smem = pl.BlockSpec(memory_space=pltpu.SMEM)
    return pl.pallas_call(
        functools.partial(body, dims),
        out_shape=jax.ShapeDtypeStruct(field.shape, f32),
        in_specs=[in_vmem] * 5 + [in_smem] * 3,
        out_specs=in_vmem,
        scratch_shapes=[
            pltpu.VMEM(phase.shape, f32),
            pltpu.VMEM(phase.shape, f32),
            pltpu.VMEM((2, fine_t * coarse_p, columns), f32),
            pltpu.VMEM((2, fine_t * coarse_p, columns), f32),
            pltpu.VMEM((fine_t, 3 * coarse_t), bf16),
            pltpu.VMEM((2, 4 * coarse_p, 4 * fine_p), bf16),
            pltpu.VMEM((coarse_t, 3 * fine_t), bf16),
            pltpu.VMEM((4 * fine_p, 8 * coarse_p), bf16),
            pltpu.VMEM((kinds + 1, 2, waves // 2, lanes), f32),
            pltpu.VMEM((members, *block), f32),
            pltpu.VMEM((3 * members, *block), f32),
            pltpu.VMEM((members, *block), f32),
            pltpu.VMEM((members, *block), f32),
            pltpu.SemaphoreType.DMA((members,)),
            pltpu.SemaphoreType.DMA((members,)),
            pltpu.SemaphoreType.DMA((2, members)),
            pltpu.SemaphoreType.DMA((2,)),
            pltpu.SemaphoreType.DMA((members,)),
            pltpu.SemaphoreType.DMA((members,)),
        ],
        compiler_params=pltpu.CompilerParams(
            collective_id=0, has_side_effects=True, vmem_limit_bytes=40 << 20
        ),
    )(field, theta, phi, phase, trans, source, kind, count)


def solution(mesh):
    groups, members = mesh.shape["grp"], mesh.shape["mem"]

    def run(field, theta, phi, phase, trans, source, kind, count):
        waves = field.shape[2] // phase.shape[0]
        return per_device(
            groups, members, waves, field, theta, phi, phase, trans, source, kind, count
        )

    return jax.shard_map(
        run,
        mesh=mesh,
        in_specs=(
            P(None, None, ("grp", "mem")),
            P(),
            P(),
            P(),
            P(None, None, "mem"),
            P("grp", None),
            P("grp", None),
            P("grp"),
        ),
        out_specs=P(None, None, ("grp", "mem")),
        check_vma=False,
    )
```

profile of v0, /device:TPU:1, one launch (start us, length us, event | category | flops | bytes accessed | tf_op | source)
XLA Modules:
  0.0 57.5 jit_solution(14217395384153879755)
XLA Ops:
  0.0 0.0 copy-start.5
  0.0 0.8 %copy.12.source_ref = s32[32,24]{1,0:T(8,128)S(1)} copy(s32[32,24]{0,1:T(8,128)} %param.13) | data formatting | bytes 6144 | tf_op args[5]
  0.8 0.0 copy-done.5
  0.8 0.0 copy-start.3
  0.8 0.1 copy.13.kind_ref
  0.9 0.6 %copy-done.3 = f32[64,32]{0,1:T(8,128)S(1)} copy-done((f32[64,32]{0,1:T(8,128)S(1)}, f32[64,32]{0,1:T(8,128)}, u32[]{:S(2)}) %copy-start.3) | copy-done | bytes 8216
  1.5 0.0 copy-start.4
  1.5 0.1 copy.9.theta_ref
  1.6 0.6 %copy-done.4 = f32[64,32]{0,1:T(8,128)S(1)} copy-done((f32[64,32]{0,1:T(8,128)S(1)}, f32[64,32]{0,1:T(8,128)}, u32[]{:S(2)}) %copy-start.4) | copy-done | bytes 8216
  2.2 0.1 copy.10.phi_ref
  2.3 0.0 copy-start.1
  2.3 0.0 copy-start.2
  2.3 1.0 %copy.11.trans_ref = f32[2,316,128]{2,1,0:T(8,128)S(1)} copy(f32[2,316,128]{2,0,1:T(2,128)} %param.12) | data formatting | bytes 647168 | tf_op args[4]
  3.4 0.0 copy-done.1
  3.4 0.0 copy-done.2
  3.4 0.0 copy-start
  3.4 1.2 %copy-done = f32[2,1024,128]{2,1,0:T(8,128)S(1)} copy-done((f32[2,1024,128]{2,1,0:T(8,128)S(1)}, f32[2,1024,128]{2,1,0:T(8,128)}, u32[]{:S(2)}) %copy-start) | copy-done | bytes 1048600
  4.6 51.9 %shard_map.82 = f32[2,1024,128]{2,1,0:T(8,128)S(1)} custom-call(f32[2,1024,128]{2,1,0:T(8,128)S(1)} %copy-done, f32[64,32]{1,0:T(8,128)S(1)} %copy.9.theta_ref, f32[64,32]{1,0:T(8,128)S(1)} %copy.10.phi_ref, f32[8,4096]{1,0:T(8,128)S(1)} %copy-done.1, f32[2,316,128]{2,1,0:T(8,128)S(1)} %copy.11.trans_ref, s32[32,24]{1,0:T(8,128)S(1)} %copy.12.source_ref, ...), custom_call_target="tpu_custom_call" | custom-call | tf_op jit(solution)/shard_map/pallas_call | solution.py:394
  56.5 1.0 %copy.15 = f32[2,1024,128]{2,1,0:T(8,128)} copy(f32[2,1024,128]{2,1,0:T(8,128)S(1)} %shard_map.82) | data formatting | bytes 2097152
Async XLA Ops:
  0.0 0.8 %copy-start.5 = (s32[32,24]{0,1:T(8,128)S(1)}, s32[32,24]{0,1:T(8,128)}, u32[]{:S(2)}) copy-start(s32[32,24]{0,1:T(8,128)} %param.14) | copy-start | bytes 9220
  0.8 0.7 %copy-start.3 = (f32[64,32]{0,1:T(8,128)S(1)}, f32[64,32]{0,1:T(8,128)}, u32[]{:S(2)}) copy-start(f32[64,32]{0,1:T(8,128)} %param.9) | copy-start | bytes 24580
  1.5 0.7 %copy-start.4 = (f32[64,32]{0,1:T(8,128)S(1)}, f32[64,32]{0,1:T(8,128)}, u32[]{:S(2)}) copy-start(f32[64,32]{0,1:T(8,128)} %param.10) | copy-start | bytes 24580
  2.3 1.1 %copy-start.1 = (f32[8,4096]{1,0:T(8,128)S(1)}, f32[8,4096]{1,0:T(8,128)}, u32[]{:S(2)}) copy-start(f32[8,4096]{1,0:T(8,128)} %phase_ref.1) | copy-start | bytes 393220
  2.3 1.1 %copy-start.2 = (s32[32]{0:T(128)S(1)}, s32[32]{0:T(128)}, u32[]{:S(2)}) copy-start(s32[32]{0:T(128)} %count_ref.1) | copy-start | bytes 388
  3.4 1.2 %copy-start = (f32[2,1024,128]{2,1,0:T(8,128)S(1)}, f32[2,1024,128]{2,1,0:T(8,128)}, u32[]{:S(2)}) copy-start(f32[2,1024,128]{2,1,0:T(8,128)} %x_ref.1) | copy-start | bytes 3145732
where the time goes:
time: 57.8 us; the launch traced here: 57.5 us
  Pallas kernels  51.9 us (90%)
  local copies, waits for them, and re-layouts  5.54 us (10%)
    pallas_call x1, Pallas kernels, per_device(): pl.pallas_call(functools.partial(body, dims), out_shape=jax.ShapeDtypeStr...  51.9 us
    unnamed x18, local copies, waits for them, and re-layouts  5.54 us

commit v1 on v0

v1 whole, which is shorter than its diff:
```python
import functools
import math

import jax
import jax.numpy as jnp
from jax import lax
from jax.experimental import pallas as pl
from jax.experimental.pallas import tpu as pltpu
from jax.sharding import PartitionSpec as P

MESH = pl.DeviceIdType.MESH
f32 = jnp.float32
bf16 = jnp.bfloat16


def two_terms(x):
    high = x.astype(bf16)
    return high, (x - high.astype(f32)).astype(bf16)


def dot(a, b):
    return jnp.dot(a, b, preferred_element_type=f32)


def dot_rows(a, b):
    return lax.dot_general(a, b, (((1,), (1,)), ((), ())), preferred_element_type=f32)


def where_true(rows, cols, test):
    r = lax.broadcasted_iota(jnp.int32, (rows, cols), 0)
    c = lax.broadcasted_iota(jnp.int32, (rows, cols), 1)
    return jnp.where(test(r, c), 1.0, 0.0).astype(f32)


def sine_and_cosine(q):
    y = 0.5 * q
    z = y * y
    s = 0.0
    for n in (11, 9, 7, 5, 3, 1):
        s = s * z + (-1.0) ** (n // 2) / math.factorial(n)
    c = 0.0
    for n in (12, 10, 8, 6, 4, 2, 0):
        c = c * z + (-1.0) ** (n // 2) / math.factorial(n)
    s = s * y
    return 2.0 * s * c, 1.0 - 2.0 * s * s


def body(
    dims,
    x_hbm,
    theta_hbm,
    phi_hbm,
    phase_hbm,
    trans_hbm,
    source_hbm,
    kind_hbm,
    count_hbm,
    out_ref,
    x_ref,
    theta_ref,
    phi_ref,
    phase_ref,
    trans_ref,
    source_ref,
    kind_ref,
    count_ref,
    place_ref,
    index_ref,
    index_sem,
    load_sem,
    cos_ref,
    sin_ref,
    mid_ref,
    turn_ref,
    back_ref,
    spread_lhs,
    spread_rhs,
    fold_lhs,
    fold_rhs,
    table_ref,
    give_ref,
    hold_first,
    hold_second,
    result_ref,
    take_ref,
    give_sem,
    hold_sem,
    pass_sem,
    side_sem,
    result_sem,
    take_sem,
):
    groups, members, coarse_t, coarse_p, fine_t, fine_p, branch, waves, slots, kinds = dims
    pairs = members // 2
    lanes = 2 * fine_p
    columns = branch * waves
    rows8 = waves // 2
    hold = (hold_first, hold_second)
    me = lax.axis_index("mem")
    group = lax.axis_index("grp")
    right = lax.rem(group + 1, groups)
    left = lax.rem(group + groups - 1, groups)

    loads = [
        pltpu.make_async_copy(src, dst, load_sem.at[n])
        for n, (src, dst) in enumerate(
            (
                (x_hbm, x_ref),
                (theta_hbm, theta_ref),
                (phi_hbm, phi_ref),
                (phase_hbm, phase_ref),
                (trans_hbm, trans_ref),
                (source_hbm, source_ref),
                (kind_hbm, kind_ref),
                (count_hbm, count_ref),
            )
        )
    ]
    for load in loads:
        load.start()

    barrier = pltpu.get_barrier_semaphore()

    def greet(k, carry):
        pl.semaphore_signal(
            barrier, inc=1, device_id={"mem": lax.rem(me + k, members)}, device_id_type=MESH
        )
        return carry

    lax.fori_loop(1, members, greet, 0)
    for other in (left, right):
        pl.semaphore_signal(barrier, inc=1, device_id={"grp": other}, device_id_type=MESH)

    def pair_at(k, sign):
        if pairs == 16:
            step = lax.rem(11 * (k + 1), 16)
            home = me // 2
            y = lax.rem(home // 4 + 4 + sign * (step // 4), 4)
            z = lax.rem(lax.rem(home, 4) + 4 + sign * lax.rem(step, 4), 4)
            return 4 * y + z
        return lax.rem(me // 2 + pairs + sign * lax.rem(k + 1, pairs), pairs)

    for load in loads[1:4]:
        load.wait()
    theta_high, theta_low = two_terms(theta_ref[...])
    phi_high, phi_low = two_terms(phi_ref[...])
    at = lambda rows, cols, test: where_true(rows, cols, test).astype(bf16)
    eye = at(fine_t, fine_t, lambda r, c: r == c)
    spread_lhs[...] = (
        dot(dot_rows(eye, theta_high).astype(bf16), at(coarse_t, 3 * coarse_t, lambda r, c: (c == r) | (c == r + coarse_t)))
        + dot(dot_rows(eye, theta_low).astype(bf16), at(coarse_t, 3 * coarse_t, lambda r, c: c == r + 2 * coarse_t))
    ).astype(bf16)
    own = where_true(4 * coarse_p, 4 * fine_p, lambda r, c: r // coarse_p == c // fine_p)
    rows_p = at(4 * coarse_p, coarse_p, lambda r, c: (r & (coarse_p - 1)) == c)
    cols_b = at(fine_p, 4 * fine_p, lambda r, c: r == (c & (fine_p - 1)))
    for n, term in enumerate((phi_high, phi_low)):
        small = dot(rows_p, term).astype(bf16)
        spread_rhs[n] = (dot(small, cols_b) * own).astype(bf16)

    def angles(i, carry):
        at_lanes = pl.ds(pl.multiple_of(i * 2 * lanes, 2 * lanes), 2 * lanes)
        s, c = sine_and_cosine(phase_ref[:, at_lanes])
        sin_ref[:, at_lanes] = s
        cos_ref[:, at_lanes] = c
        return carry

    lax.fori_loop(0, pairs, angles, 0)

    for load in loads[5:]:
        load.wait()

    used = lax.broadcasted_iota(jnp.int32, (slots, members), 0) < count_ref[...]
    place_ref[0] = jnp.where(used, source_ref[...] - (group - 1) * members, members)
    place_ref[1] = jnp.where(used, kind_ref[...], kinds)
    places = pltpu.make_async_copy(place_ref, index_ref, index_sem)
    places.start()

    lhs = spread_lhs[...]
    loads[0].wait()

    def theta_step(p, carry):
        terms = [two_terms(x_ref[n, pl.ds(p, coarse_t, stride=coarse_p), :]) for n in range(2)]
        high = jnp.concatenate([terms[0][0], terms[1][0]], axis=1)
        low = jnp.concatenate([terms[0][1], terms[1][1]], axis=1)
        made = dot(lhs, jnp.concatenate([high, low, high], axis=0))
        for n in range(2):
            mid_ref[n, pl.ds(p, fine_t, stride=coarse_p), :] = made[
                :, n * columns : (n + 1) * columns
            ]
        return carry

    lax.fori_loop(0, coarse_p, theta_step, 0, unroll=8)

    pl.semaphore_wait(barrier, members + 1)

    def give_copy(half, to):
        return pltpu.make_async_remote_copy(
            src_ref=give_ref.at[half, to],
            dst_ref=hold[half].at[members + me],
            send_sem=give_sem.at[half],
            recv_sem=hold_sem.at[half, me // 2],
            device_id={"mem": to},
            device_id_type=MESH,
        )

    def spread_pair(home, k, carry):
        pair = pair_at(k, 1)
        rows = pl.ds(pl.multiple_of(pair * 4 * coarse_p, 4 * coarse_p), 4 * coarse_p)
        turned = jnp.concatenate([mid_ref[0, rows, :].T, mid_ref[1, rows, :].T], axis=0)
        high, low = two_terms(turned)
        both = jnp.concatenate([spread_rhs[0], spread_rhs[0]], axis=0)
        fine = dot(jnp.concatenate([high, low], axis=1), both) + dot(high, spread_rhs[1])
        at_lanes = pl.ds(pl.multiple_of(pair * 2 * lanes, 2 * lanes), 2 * lanes)
        cosine = cos_ref[:, at_lanes]
        sine = sin_ref[:, at_lanes]
        real = imag = 0.0
        for j in range(branch):
            re = fine[j * waves : (j + 1) * waves]
            im = fine[columns + j * waves : columns + (j + 1) * waves]
            c, s = cosine[j : j + 1], sine[j : j + 1]
            real = real + (re * c - im * s)
            imag = imag + (im * c + re * s)
        for side in range(2):
            to = 2 * pair + side
            for half in range(2):
                for n, part in enumerate((real, imag)):
                    give_ref[half, to, n] = part[
                        half * rows8 : (half + 1) * rows8, side * lanes : (side + 1) * lanes
                    ]

            if not home:
                give_copy(0, to).start()
        return carry

    other = me + 1 - 2 * lax.rem(me, 2)
    lax.fori_loop(0, pairs - 1, functools.partial(spread_pair, False), 0, unroll=3)
    spread_pair(True, pairs - 1, 0)
    give_copy(0, other).start()
    for half in range(2):
        hold[half][members + me] = give_ref[half, me]

    def give_rest(k, carry):
        for side in range(2):
            give_copy(1, 2 * pair_at(k, 1) + side).start()
        return carry

    lax.fori_loop(0, pairs - 1, give_rest, 0)
    give_copy(1, other).start()

    loads[4].wait()

    def table_step(i, carry):
        for n in range(2):
            table_ref[i, n] = jnp.broadcast_to(trans_ref[i, pl.ds(n, 1), :], (rows8, lanes))
        return carry

    lax.fori_loop(0, kinds, table_step, 0, unroll=4)
    table_ref[kinds] = jnp.zeros((2, rows8, lanes), f32)

    own_back = where_true(4 * fine_p, 4 * coarse_p, lambda r, c: r // fine_p == c // coarse_p)
    rows_b = at(4 * fine_p, fine_p, lambda r, c: (r & (fine_p - 1)) == c)
    cols_p = at(coarse_p, 4 * coarse_p, lambda r, c: r == (c & (coarse_p - 1)))
    for n, term in enumerate((phi_high, phi_low)):
        small = dot_rows(rows_b, term).astype(bf16)
        fold_rhs[:, n * 4 * coarse_p : (n + 1) * 4 * coarse_p] = (
            dot(small, cols_p) * own_back
        ).astype(bf16)
    fold_lhs[...] = (
        dot(theta_high, at(fine_t, 3 * fine_t, lambda r, c: (c == r) | (c == r + fine_t)))
        + dot(theta_low, at(fine_t, 3 * fine_t, lambda r, c: c == r + 2 * fine_t))
    ).astype(bf16)
    places.wait()

    def pass_copy(half, first, count, way):
        to = right if way == 0 else left
        return pltpu.make_async_remote_copy(
            src_ref=hold[half].at[pl.ds(members + first, count)],
            dst_ref=hold[half].at[pl.ds(2 * members * way + first, count)],
            send_sem=pass_sem.at[half, way],
            recv_sem=side_sem.at[half, way],
            device_id={"grp": to},
            device_id_type=MESH,
        )

    def result_copy(half, target):
        return pltpu.make_async_remote_copy(
            src_ref=result_ref.at[half, target],
            dst_ref=take_ref.at[half, me],
            send_sem=result_sem.at[half],
            recv_sem=take_sem.at[half, me // 2],
            device_id={"mem": target},
            device_id_type=MESH,
        )

    def landed(ref, sem, pair):
        def wait(count):
            pltpu.make_async_remote_copy(
                src_ref=ref.at[pl.ds(0, count)],
                dst_ref=ref.at[pl.ds(0, count)],
                send_sem=give_sem.at[0],
                recv_sem=sem,
                device_id={"mem": other},
                device_id_type=MESH,
            ).wait_recv()

        @pl.when(pair != me // 2)
        def _():
            wait(2)

        @pl.when(pair == me // 2)
        def _():
            wait(1)

    def pass_order(k):
        if pairs == 16:
            return 4 * lax.rem(k, 4) + k // 4
        return k

    for half in range(2):

        def pass_pair(k, carry):
            pair = pass_order(k)
            landed(hold[half].at[pl.ds(members, members)], hold_sem.at[half, pair], pair)
            for way in range(2):
                pass_copy(half, 2 * pair, 2, way).start()
            return carry

        lax.fori_loop(0, pairs, pass_pair, 0)

        for way in range(2):
            span = hold[half].at[pl.ds(2 * members * way, members)]
            pltpu.make_async_remote_copy(
                src_ref=span,
                dst_ref=span,
                send_sem=pass_sem.at[half, way],
                recv_sem=side_sem.at[half, way],
                device_id={"grp": right},
                device_id_type=MESH,
            ).wait_recv()

        def translate(target, away):
            real = jnp.zeros((rows8, lanes), f32)
            imag = jnp.zeros((rows8, lanes), f32)
            for slot in range(slots):
                box = hold[half][index_ref[0, slot, target]]
                factor = table_ref[index_ref[1, slot, target]]
                real = real + (factor[0] * box[0] - factor[1] * box[1])
                imag = imag + (factor[0] * box[1] + factor[1] * box[0])
            if away:
                result_ref[half, target, 0] = real
                result_ref[half, target, 1] = imag
                result_copy(half, target).start()
            else:
                take_ref[half, me, 0] = real
                take_ref[half, me, 1] = imag

        def translate_pair(k, carry):
            for side in range(2):
                translate(2 * pair_at(k, 1) + side, True)
            return carry

        lax.fori_loop(0, pairs - 1, translate_pair, 0)
        translate(other, True)
        translate(me, False)

    width = 4 * coarse_p
    for half in range(2):

        def fold_pair(home, k, carry):
            pair = pair_at(k, -1)
            if home:
                landed(take_ref.at[half], take_sem.at[half, pair], pair)
            else:
                two = take_ref.at[half, pl.ds(0, 2)]
                pltpu.make_async_remote_copy(
                    src_ref=two,
                    dst_ref=two,
                    send_sem=give_sem.at[0],
                    recv_sem=take_sem.at[half, pair],
                    device_id={"mem": other},
                    device_id_type=MESH,
                ).wait_recv()
            at_lanes = pl.ds(pl.multiple_of(pair * 2 * lanes, 2 * lanes), 2 * lanes)
            cosine = cos_ref[:, at_lanes]
            sine = sin_ref[:, at_lanes]
            re, im = (
                jnp.concatenate([take_ref[half, 2 * pair + side, n] for side in range(2)], axis=1)
                for n in range(2)
            )
            parts = [[], []]
            for j in range(branch):
                c, s = cosine[j : j + 1], sine[j : j + 1]
                parts[0].append(re * c + im * s)
                parts[1].append(im * c - re * s)
            high, low = two_terms(jnp.concatenate(parts[0] + parts[1], axis=0))
            wide = dot(high, fold_rhs[...])
            made = wide[:, :width] + wide[:, width:] + dot(low, fold_rhs[:, :width])
            for n in range(2):
                for j in range(branch):
                    first = (n * branch + j) * rows8
                    turn_ref[pair, n, j * waves + half * rows8 : j * waves + (half + 1) * rows8] = (
                        made[first : first + rows8]
                    )
            if half == 1:
                rows = pl.ds(pl.multiple_of(pair * width, width), width)
                for n in range(2):
                    back_ref[n, rows, :] = turn_ref[pair, n].T
            return carry

        fold_pair(True, pairs - 1, 0)
        lax.fori_loop(0, pairs - 1, functools.partial(fold_pair, False), 0, unroll=3)

    lhs_back = fold_lhs[...]

    def fold_step(p, carry):
        terms = [two_terms(back_ref[n, pl.ds(p, fine_t, stride=coarse_p), :]) for n in range(2)]
        high = jnp.concatenate([terms[0][0], terms[1][0]], axis=1)
        low = jnp.concatenate([terms[0][1], terms[1][1]], axis=1)
        made = dot(lhs_back, jnp.concatenate([high, low, high], axis=0))
        for n in range(2):
            out_ref[n, pl.ds(p, coarse_t, stride=coarse_p), :] = made[
                :, n * columns : (n + 1) * columns
            ]
        return carry

    lax.fori_loop(0, coarse_p, fold_step, 0, unroll=8)

    def left_here(ref, sem):
        pltpu.make_async_remote_copy(
            src_ref=ref,
            dst_ref=ref,
            send_sem=sem,
            recv_sem=take_sem.at[0, 0],
            device_id={"mem": other},
            device_id_type=MESH,
        ).wait_send()

    for half in range(2):
        left_here(give_ref.at[half, pl.ds(0, members - 1)], give_sem.at[half])
        left_here(result_ref.at[half, pl.ds(0, members - 1)], result_sem.at[half])
        for way in range(2):
            left_here(hold[half].at[pl.ds(0, members)], pass_sem.at[half, way])


def per_device(groups, members, waves, *arrays):
    field, theta, phi, phase, trans, source, kind, count = arrays
    theta, phi, trans = theta.T, phi.T, trans.transpose(1, 0, 2)
    source, kind, count = source.T, kind.T, count.reshape(1, -1)
    coarse_t, fine_t = theta.shape
    coarse_p, fine_p = phi.shape
    branch = phase.shape[0]
    slots = source.shape[0]
    kinds = trans.shape[0]
    columns = field.shape[2]
    lanes = trans.shape[2]
    dims = (groups, members, coarse_t, coarse_p, fine_t, fine_p, branch, waves, slots, kinds)
    block = (2, waves // 2, lanes)
    return pl.pallas_call(
        functools.partial(body, dims),
        out_shape=jax.ShapeDtypeStruct(field.shape, f32),
        in_specs=[pl.BlockSpec(memory_space=pltpu.HBM)] * 8,
        out_specs=pl.BlockSpec(memory_space=pltpu.VMEM),
        scratch_shapes=[
            *(pltpu.VMEM(a.shape, f32) for a in (field, theta, phi, phase, trans)),
            *(pltpu.VMEM(a.shape, jnp.int32) for a in (source, kind, count)),
            pltpu.VMEM((2, slots, members), jnp.int32),
            pltpu.SMEM((2, slots, members), jnp.int32),
            pltpu.SemaphoreType.DMA,
            pltpu.SemaphoreType.DMA((8,)),
            pltpu.VMEM(phase.shape, f32),
            pltpu.VMEM(phase.shape, f32),
            pltpu.VMEM((2, fine_t * coarse_p, columns), f32),
            pltpu.VMEM((members // 2, 2, columns, 4 * coarse_p), f32),
            pltpu.VMEM((2, fine_t * coarse_p, columns), f32),
            pltpu.VMEM((fine_t, 3 * coarse_t), bf16),
            pltpu.VMEM((2, 4 * coarse_p, 4 * fine_p), bf16),
            pltpu.VMEM((coarse_t, 3 * fine_t), bf16),
            pltpu.VMEM((4 * fine_p, 8 * coarse_p), bf16),
            pltpu.VMEM((kinds + 1, 2, waves // 2, lanes), f32),
            pltpu.VMEM((2, members, *block), f32),
            pltpu.VMEM((3 * members, *block), f32),
            pltpu.VMEM((3 * members, *block), f32),
            pltpu.VMEM((2, members, *block), f32),
            pltpu.VMEM((2, members, *block), f32),
            pltpu.SemaphoreType.DMA((2,)),
            pltpu.SemaphoreType.DMA((2, members // 2)),
            pltpu.SemaphoreType.DMA((2, 2)),
            pltpu.SemaphoreType.DMA((2, 2)),
            pltpu.SemaphoreType.DMA((2,)),
            pltpu.SemaphoreType.DMA((2, members // 2)),
        ],
        compiler_params=pltpu.CompilerParams(
            collective_id=0, has_side_effects=True, vmem_limit_bytes=40 << 20
        ),
    )(*(pltpu.with_memory_space_constraint(a, pltpu.HBM) for a in (field, theta, phi, phase, trans, source, kind, count)))


def solution(mesh):
    groups, members = mesh.shape["grp"], mesh.shape["mem"]

    def run(field, theta, phi, phase, trans, source, kind, count):
        waves = field.shape[2] // phase.shape[0]
        return per_device(
            groups, members, waves, field, theta, phi, phase, trans, source, kind, count
        )

    return jax.shard_map(
        run,
        mesh=mesh,
        in_specs=(
            P(None, None, ("grp", "mem")),
            P(),
            P(),
            P(),
            P(None, None, "mem"),
            P("grp", None),
            P("grp", None),
            P("grp"),
        ),
        out_specs=P(None, None, ("grp", "mem")),
        check_vma=False,
    )
```

time: 57.8 us -> 47.9 us (0.83)
  the two profiles are of different devices: /device:TPU:1 before, /device:TPU:7 now
where the time goes in v1:
time: 47.9 us; the launch traced here: 47.8 us
  Pallas kernels  46.9 us (98%)
  local copies, waits for them, and re-layouts  0.97 us (2%)
    pallas_call x1, Pallas kernels, per_device(): pl.pallas_call(functools.partial(body, dims), out_shape=jax.ShapeDtypeStr...  46.9 us
    unnamed x1, local copies, waits for them, and re-layouts  0.97 us

profile of v1, /device:TPU:7, one launch (start us, length us, event | category | flops | bytes accessed | tf_op | source)
XLA Modules:
  0.0 47.8 jit_solution(8273349130810727170)
XLA Ops:
  0.0 46.9 %shard_map.82 = f32[2,1024,128]{2,1,0:T(8,128)S(1)} custom-call(f32[2,1024,128]{2,1,0:T(8,128)} %x_hbm.1, f32[32,64]{1,0:T(8,128)} %bitcast.7, f32[32,64]{1,0:T(8,128)} %bitcast.8, f32[8,4096]{1,0:T(8,128)} %phase_hbm.1, f32[316,2,128]{2,1,0:T(2,128)} %bitcast.6, s32[24,32]{1,0:T(8,128)} %bitcast.9, s32[24,32]{1,0:T(8,128)} %bitcast.10, s32[1,32]{1,0:T(1,128)} %bitcast.11), custom_call_target="tpu_custom_call" | custom-call | tf_op jit(solution)/shard_map/pallas_call | solution.py:458
  46.9 1.0 %copy.10 = f32[2,1024,128]{2,1,0:T(8,128)} copy(f32[2,1024,128]{2,1,0:T(8,128)S(1)} %shard_map.82) | data formatting | bytes 2097152

commit v2 on v1

--- a/solution.py
+++ b/solution.py
@@ -79,8 +79,8 @@
     fold_rhs,
     table_ref,
     give_ref,
-    hold_first,
-    hold_second,
+    hold_0,
+    hold_1,
     result_ref,
     take_ref,
     give_sem,
@@ -94,8 +94,11 @@
     pairs = members // 2
     lanes = 2 * fine_p
     columns = branch * waves
-    rows8 = waves // 2
-    hold = (hold_first, hold_second)
+    hold = (hold_0, hold_1)
+    chunks = len(hold)
+    few = waves // chunks
+    half_waves = waves // 2
+    chunks_of = lambda half: range(half * chunks // 2, (half + 1) * chunks // 2)
     me = lax.axis_index("mem")
     group = lax.axis_index("grp")
     right = lax.rem(group + 1, groups)
@@ -131,14 +134,15 @@
     for other in (left, right):
         pl.semaphore_signal(barrier, inc=1, device_id={"grp": other}, device_id_type=MESH)
 
+    home_pair = me // 2
+    row = members // 4
+
     def pair_at(k, sign):
-        if pairs == 16:
-            step = lax.rem(11 * (k + 1), 16)
-            home = me // 2
-            y = lax.rem(home // 4 + 4 + sign * (step // 4), 4)
-            z = lax.rem(lax.rem(home, 4) + 4 + sign * lax.rem(step, 4), 4)
-            return 4 * y + z
-        return lax.rem(me // 2 + pairs + sign * lax.rem(k + 1, pairs), pairs)
+        if sign == 1:
+            up = home_pair + (k + 1)
+            return jnp.where(up >= pairs, up - pairs, up)
+        down = home_pair - (k + 1)
+        return jnp.where(down < 0, down + pairs, down)
 
     for load in loads[1:4]:
         load.wait()
@@ -189,7 +193,7 @@
             ]
         return carry
 
-    lax.fori_loop(0, coarse_p, theta_step, 0, unroll=8)
+    lax.fori_loop(0, coarse_p, theta_step, 0, unroll=32)
 
     pl.semaphore_wait(barrier, members + 1)
 
@@ -198,7 +202,7 @@
             src_ref=give_ref.at[half, to],
             dst_ref=hold[half].at[members + me],
             send_sem=give_sem.at[half],
-            recv_sem=hold_sem.at[half, me // 2],
+            recv_sem=hold_sem.at[half, me // row],
             device_id={"mem": to},
             device_id_type=MESH,
         )
@@ -222,11 +226,14 @@
             imag = imag + (im * c + re * s)
         for side in range(2):
             to = 2 * pair + side
-            for half in range(2):
-                for n, part in enumerate((real, imag)):
-                    give_ref[half, to, n] = part[
-                        half * rows8 : (half + 1) * rows8, side * lanes : (side + 1) * lanes
-                    ]
+            for chunk in range(chunks):
+                give_ref[chunk, to] = jnp.concatenate(
+                    [
+                        part[chunk * few : (chunk + 1) * few, side * lanes : (side + 1) * lanes]
+                        for part in (real, imag)
+                    ],
+                    axis=0,
+                )
 
             if not home:
                 give_copy(0, to).start()
@@ -236,26 +243,31 @@
     lax.fori_loop(0, pairs - 1, functools.partial(spread_pair, False), 0, unroll=3)
     spread_pair(True, pairs - 1, 0)
     give_copy(0, other).start()
-    for half in range(2):
-        hold[half][members + me] = give_ref[half, me]
-
-    def give_rest(k, carry):
-        for side in range(2):
-            give_copy(1, 2 * pair_at(k, 1) + side).start()
-        return carry
-
-    lax.fori_loop(0, pairs - 1, give_rest, 0)
-    give_copy(1, other).start()
+    for chunk in range(chunks):
+        hold[chunk][members + me] = give_ref[chunk, me]
+
+    for chunk in range(1, chunks):
+
+        def give_rest(k, carry):
+            for side in range(2):
+                give_copy(chunk, 2 * pair_at(k, 1) + side).start()
+            return carry
+
+        lax.fori_loop(0, pairs - 1, give_rest, 0)
+        give_copy(chunk, other).start()
 
     loads[4].wait()
+
+    signs = jnp.where(lax.broadcasted_iota(jnp.int32, (2 * few, lanes), 0) < few, 1.0, -1.0)
 
     def table_step(i, carry):
         for n in range(2):
-            table_ref[i, n] = jnp.broadcast_to(trans_ref[i, pl.ds(n, 1), :], (rows8, lanes))
+            row = jnp.broadcast_to(trans_ref[i, pl.ds(n, 1), :], (2 * few, lanes))
+            table_ref[i, n] = row if n == 0 else row * signs
         return carry
 
     lax.fori_loop(0, kinds, table_step, 0, unroll=4)
-    table_ref[kinds] = jnp.zeros((2, rows8, lanes), f32)
+    table_ref[kinds] = jnp.zeros((2, 2 * few, lanes), f32)
 
     own_back = where_true(4 * fine_p, 4 * coarse_p, lambda r, c: r // fine_p == c // coarse_p)
     rows_b = at(4 * fine_p, fine_p, lambda r, c: (r & (fine_p - 1)) == c)
@@ -287,46 +299,36 @@
             src_ref=result_ref.at[half, target],
             dst_ref=take_ref.at[half, me],
             send_sem=result_sem.at[half],
-            recv_sem=take_sem.at[half, me // 2],
+            recv_sem=take_sem.at[half, me // 2 if half == chunks - 1 else 0],
             device_id={"mem": target},
             device_id_type=MESH,
         )
 
-    def landed(ref, sem, pair):
-        def wait(count):
-            pltpu.make_async_remote_copy(
-                src_ref=ref.at[pl.ds(0, count)],
-                dst_ref=ref.at[pl.ds(0, count)],
-                send_sem=give_sem.at[0],
-                recv_sem=sem,
-                device_id={"mem": other},
-                device_id_type=MESH,
-            ).wait_recv()
-
-        @pl.when(pair != me // 2)
+    def blocks_landed(ref, sem, count):
+        some = ref.at[pl.ds(0, count)]
+        pltpu.make_async_remote_copy(
+            src_ref=some,
+            dst_ref=some,
+            send_sem=give_sem.at[0],
+            recv_sem=sem,
+            device_id={"mem": other},
+            device_id_type=MESH,
+        ).wait_recv()
+
+    def pass_row(half, k, carry):
+        @pl.when(k == me // row)
         def _():
-            wait(2)
-
-        @pl.when(pair == me // 2)
+            blocks_landed(hold[half], hold_sem.at[half, k], row - 1)
+
+        @pl.when(k != me // row)
         def _():
-            wait(1)
-
-    def pass_order(k):
-        if pairs == 16:
-            return 4 * lax.rem(k, 4) + k // 4
-        return k
-
-    for half in range(2):
-
-        def pass_pair(k, carry):
-            pair = pass_order(k)
-            landed(hold[half].at[pl.ds(members, members)], hold_sem.at[half, pair], pair)
-            for way in range(2):
-                pass_copy(half, 2 * pair, 2, way).start()
-            return carry
-
-        lax.fori_loop(0, pairs, pass_pair, 0)
-
+            blocks_landed(hold[half], hold_sem.at[half, k], row)
+
+        for way in range(2):
+            pass_copy(half, row * k, row, way).start()
+        return carry
+
+    def sides_landed(half):
         for way in range(2):
             span = hold[half].at[pl.ds(2 * members * way, members)]
             pltpu.make_async_remote_copy(
@@ -338,53 +340,68 @@
                 device_id_type=MESH,
             ).wait_recv()
 
-        def translate(target, away):
-            real = jnp.zeros((rows8, lanes), f32)
-            imag = jnp.zeros((rows8, lanes), f32)
-            for slot in range(slots):
-                box = hold[half][index_ref[0, slot, target]]
-                factor = table_ref[index_ref[1, slot, target]]
-                real = real + (factor[0] * box[0] - factor[1] * box[1])
-                imag = imag + (factor[0] * box[1] + factor[1] * box[0])
-            if away:
-                result_ref[half, target, 0] = real
-                result_ref[half, target, 1] = imag
-                result_copy(half, target).start()
-            else:
-                take_ref[half, me, 0] = real
-                take_ref[half, me, 1] = imag
-
-        def translate_pair(k, carry):
-            for side in range(2):
-                translate(2 * pair_at(k, 1) + side, True)
-            return carry
-
-        lax.fori_loop(0, pairs - 1, translate_pair, 0)
-        translate(other, True)
-        translate(me, False)
+    def translate(half, target, away):
+        straight = jnp.zeros((2 * few, lanes), f32)
+        crossed = jnp.zeros((2 * few, lanes), f32)
+        for slot in range(slots):
+            box = hold[half][index_ref[0, slot, target]]
+            factor = table_ref[index_ref[1, slot, target]]
+            straight = straight + factor[0] * box
+            crossed = crossed + factor[1] * box
+        made = straight + jnp.concatenate([crossed[few:], crossed[:few]], axis=0)
+        if away:
+            result_ref[half, target] = made
+            result_copy(half, target).start()
+        else:
+            take_ref[half, me] = made
+
+    def translate_pair(half, k, carry):
+        for side in range(2):
+            translate(half, 2 * pair_at(k, 1) + side, True)
+        return carry
+
+    def pass_rows(chunk, first, end):
+        lax.fori_loop(first, end, functools.partial(pass_row, chunk), 0)
+
+    def translate_all(chunk):
+        lax.fori_loop(0, pairs - 1, functools.partial(translate_pair, chunk), 0)
+        translate(chunk, other, True)
+        translate(chunk, me, False)
+
+    rows = members // row
+    pass_rows(0, 0, rows)
+    pass_rows(1, 0, rows - 1)
+    sides_landed(0)
+    translate_all(0)
+    pass_rows(1, rows - 1, rows)
+    sides_landed(1)
+    translate_all(1)
 
     width = 4 * coarse_p
     for half in range(2):
 
         def fold_pair(home, k, carry):
             pair = pair_at(k, -1)
-            if home:
-                landed(take_ref.at[half], take_sem.at[half, pair], pair)
-            else:
-                two = take_ref.at[half, pl.ds(0, 2)]
-                pltpu.make_async_remote_copy(
-                    src_ref=two,
-                    dst_ref=two,
-                    send_sem=give_sem.at[0],
-                    recv_sem=take_sem.at[half, pair],
-                    device_id={"mem": other},
-                    device_id_type=MESH,
-                ).wait_recv()
+            if half == 1:
+                last = chunks - 1
+                blocks_landed(take_ref.at[last], take_sem.at[last, pair], 1 if home else 2)
             at_lanes = pl.ds(pl.multiple_of(pair * 2 * lanes, 2 * lanes), 2 * lanes)
             cosine = cos_ref[:, at_lanes]
             sine = sin_ref[:, at_lanes]
             re, im = (
-                jnp.concatenate([take_ref[half, 2 * pair + side, n] for side in range(2)], axis=1)
+                jnp.concatenate(
+                    [
+                        jnp.concatenate(
+                            [
+                                take_ref[chunk, 2 * pair + side, n * few : (n + 1) * few]
+                                for chunk in chunks_of(half)
+                            ],
+                            axis=0,
+                        )
+                        for side in range(2)
+                    ],
+                    axis=1,
+                )
                 for n in range(2)
             )
             parts = [[], []]
@@ -397,18 +414,20 @@
             made = wide[:, :width] + wide[:, width:] + dot(low, fold_rhs[:, :width])
             for n in range(2):
                 for j in range(branch):
-                    first = (n * branch + j) * rows8
-                    turn_ref[pair, n, j * waves + half * rows8 : j * waves + (half + 1) * rows8] = (
-                        made[first : first + rows8]
-                    )
+                    first = (n * branch + j) * half_waves
+                    to = j * waves + half * half_waves
+                    turn_ref[pair, n, to : to + half_waves] = made[first : first + half_waves]
             if half == 1:
                 rows = pl.ds(pl.multiple_of(pair * width, width), width)
                 for n in range(2):
                     back_ref[n, rows, :] = turn_ref[pair, n].T
             return carry
 
+        for chunk in chunks_of(half):
+            if chunk < chunks - 1:
+                blocks_landed(take_ref.at[chunk], take_sem.at[chunk, 0], members - 1)
+        lax.fori_loop(0, pairs - 1, functools.partial(fold_pair, False), 0, unroll=3)
         fold_pair(True, pairs - 1, 0)
-        lax.fori_loop(0, pairs - 1, functools.partial(fold_pair, False), 0, unroll=3)
 
     lhs_back = fold_lhs[...]
 
@@ -423,7 +442,7 @@
             ]
         return carry
 
-    lax.fori_loop(0, coarse_p, fold_step, 0, unroll=8)
+    lax.fori_loop(0, coarse_p, fold_step, 0, unroll=32)
 
     def left_here(ref, sem):
         pltpu.make_async_remote_copy(
@@ -435,7 +454,7 @@
             device_id_type=MESH,
         ).wait_send()
 
-    for half in range(2):
+    for half in range(chunks):
         left_here(give_ref.at[half, pl.ds(0, members - 1)], give_sem.at[half])
         left_here(result_ref.at[half, pl.ds(0, members - 1)], result_sem.at[half])
         for way in range(2):
@@ -454,7 +473,8 @@
     columns = field.shape[2]
     lanes = trans.shape[2]
     dims = (groups, members, coarse_t, coarse_p, fine_t, fine_p, branch, waves, slots, kinds)
-    block = (2, waves // 2, lanes)
+    chunks = 2
+    block = (2 * (waves // chunks), lanes)
     return pl.pallas_call(
         functools.partial(body, dims),
         out_shape=jax.ShapeDtypeStruct(field.shape, f32),
@@ -476,18 +496,17 @@
             pltpu.VMEM((2, 4 * coarse_p, 4 * fine_p), bf16),
             pltpu.VMEM((coarse_t, 3 * fine_t), bf16),
             pltpu.VMEM((4 * fine_p, 8 * coarse_p), bf16),
-            pltpu.VMEM((kinds + 1, 2, waves // 2, lanes), f32),
-            pltpu.VMEM((2, members, *block), f32),
-            pltpu.VMEM((3 * members, *block), f32),
-            pltpu.VMEM((3 * members, *block), f32),
-            pltpu.VMEM((2, members, *block), f32),
-            pltpu.VMEM((2, members, *block), f32),
-            pltpu.SemaphoreType.DMA((2,)),
-            pltpu.SemaphoreType.DMA((2, members // 2)),
-            pltpu.SemaphoreType.DMA((2, 2)),
-            pltpu.SemaphoreType.DMA((2, 2)),
-            pltpu.SemaphoreType.DMA((2,)),
-            pltpu.SemaphoreType.DMA((2, members // 2)),
+            pltpu.VMEM((kinds + 1, 2, *block), f32),
+            pltpu.VMEM((chunks, members, *block), f32),
+            *(pltpu.VMEM((3 * members, *block), f32) for _ in range(chunks)),
+            pltpu.VMEM((chunks, members, *block), f32),
+            pltpu.VMEM((chunks, members, *block), f32),
+            pltpu.SemaphoreType.DMA((chunks,)),
+            pltpu.SemaphoreType.DMA((chunks, 4)),
+            pltpu.SemaphoreType.DMA((chunks, 2)),
+            pltpu.SemaphoreType.DMA((chunks, 2)),
+            pltpu.SemaphoreType.DMA((chunks,)),
+            pltpu.SemaphoreType.DMA((chunks, members // 2)),
         ],
         compiler_params=pltpu.CompilerParams(
             collective_id=0, has_side_effects=True, vmem_limit_bytes=40 << 20

time: 47.9 us -> 46.8 us (0.977)
  the two profiles are of different devices: /device:TPU:7 before, /device:TPU:1 now
where the time goes in v2:
time: 46.8 us; the launch traced here: 46.7 us
  Pallas kernels  45.7 us (98%)
  local copies, waits for them, and re-layouts  0.97 us (2%)
    pallas_call x1, Pallas kernels, per_device(): pl.pallas_call(functools.partial(body, dims), out_shape=jax.ShapeDtypeStr...  45.7 us
    unnamed x1, local copies, waits for them, and re-layouts  0.97 us

profile of v2, /device:TPU:1, one launch (start us, length us, event | category | flops | bytes accessed | tf_op | source)
XLA Modules:
  0.0 46.7 jit_solution(17699940819340392722)
XLA Ops:
  0.0 45.7 %shard_map.82 = f32[2,1024,128]{2,1,0:T(8,128)S(1)} custom-call(f32[2,1024,128]{2,1,0:T(8,128)} %x_hbm.1, f32[32,64]{1,0:T(8,128)} %bitcast.7, f32[32,64]{1,0:T(8,128)} %bitcast.8, f32[8,4096]{1,0:T(8,128)} %phase_hbm.1, f32[316,2,128]{2,1,0:T(2,128)} %bitcast.6, s32[24,32]{1,0:T(8,128)} %bitcast.9, s32[24,32]{1,0:T(8,128)} %bitcast.10, s32[1,32]{1,0:T(1,128)} %bitcast.11), custom_call_target="tpu_custom_call" | custom-call | tf_op jit(solution)/shard_map/pallas_call | solution.py:478
  45.7 1.0 %copy.10 = f32[2,1024,128]{2,1,0:T(8,128)} copy(f32[2,1024,128]{2,1,0:T(8,128)S(1)} %shard_map.82) | data formatting | bytes 2097152

commit v3 on v2

--- a/solution.py
+++ b/solution.py
@@ -170,15 +170,6 @@
 
     lax.fori_loop(0, pairs, angles, 0)
 
-    for load in loads[5:]:
-        load.wait()
-
-    used = lax.broadcasted_iota(jnp.int32, (slots, members), 0) < count_ref[...]
-    place_ref[0] = jnp.where(used, source_ref[...] - (group - 1) * members, members)
-    place_ref[1] = jnp.where(used, kind_ref[...], kinds)
-    places = pltpu.make_async_copy(place_ref, index_ref, index_sem)
-    places.start()
-
     lhs = spread_lhs[...]
     loads[0].wait()
 
@@ -256,6 +247,15 @@
         lax.fori_loop(0, pairs - 1, give_rest, 0)
         give_copy(chunk, other).start()
 
+    for load in loads[5:]:
+        load.wait()
+
+    used = lax.broadcasted_iota(jnp.int32, (slots, members), 0) < count_ref[...]
+    place_ref[0] = jnp.where(used, source_ref[...] - (group - 1) * members, members)
+    place_ref[1] = jnp.where(used, kind_ref[...], kinds)
+    places = pltpu.make_async_copy(place_ref, index_ref, index_sem)
+    places.start()
+
     loads[4].wait()
 
     signs = jnp.where(lax.broadcasted_iota(jnp.int32, (2 * few, lanes), 0) < few, 1.0, -1.0)
@@ -364,7 +364,7 @@
         lax.fori_loop(first, end, functools.partial(pass_row, chunk), 0)
 
     def translate_all(chunk):
-        lax.fori_loop(0, pairs - 1, functools.partial(translate_pair, chunk), 0)
+        lax.fori_loop(0, pairs - 1, functools.partial(translate_pair, chunk), 0, unroll=3)
         translate(chunk, other, True)
         translate(chunk, me, False)
 
@@ -426,7 +426,7 @@
         for chunk in chunks_of(half):
             if chunk < chunks - 1:
                 blocks_landed(take_ref.at[chunk], take_sem.at[chunk, 0], members - 1)
-        lax.fori_loop(0, pairs - 1, functools.partial(fold_pair, False), 0, unroll=3)
+        lax.fori_loop(0, pairs - 1, functools.partial(fold_pair, False), 0, unroll=5)
         fold_pair(True, pairs - 1, 0)
 
     lhs_back = fold_lhs[...]

time: 46.8 us -> 46.8 us (level)
  no operation moved by 1% of the time
where the time goes in v3:
time: 46.8 us; the launch traced here: 46.7 us
  Pallas kernels  45.8 us (98%)
  local copies, waits for them, and re-layouts  0.97 us (2%)
    pallas_call x1, Pallas kernels, per_device(): pl.pallas_call(functools.partial(body, dims), out_shape=jax.ShapeDtypeStr...  45.8 us
    unnamed x1, local copies, waits for them, and re-layouts  0.97 us

profile of v3, /device:TPU:1, one launch (start us, length us, event | category | flops | bytes accessed | tf_op | source)
XLA Modules:
  0.0 46.7 jit_solution(4551031247099398676)
XLA Ops:
  0.0 45.8 %shard_map.82 = f32[2,1024,128]{2,1,0:T(8,128)S(1)} custom-call(f32[2,1024,128]{2,1,0:T(8,128)} %x_hbm.1, f32[32,64]{1,0:T(8,128)} %bitcast.7, f32[32,64]{1,0:T(8,128)} %bitcast.8, f32[8,4096]{1,0:T(8,128)} %phase_hbm.1, f32[316,2,128]{2,1,0:T(2,128)} %bitcast.6, s32[24,32]{1,0:T(8,128)} %bitcast.9, s32[24,32]{1,0:T(8,128)} %bitcast.10, s32[1,32]{1,0:T(1,128)} %bitcast.11), custom_call_target="tpu_custom_call" | custom-call | tf_op jit(solution)/shard_map/pallas_call | solution.py:478
  45.8 1.0 %copy.10 = f32[2,1024,128]{2,1,0:T(8,128)} copy(f32[2,1024,128]{2,1,0:T(8,128)S(1)} %shard_map.82) | data formatting | bytes 2097152
